TPU v7x, 128 devices: a whole 4x4x4 slice. The times are simulated.
128 devices in a mesh: dp: 16 (over x_lo, z, core), tensor: 8 (over y, x_hi).
Axes of the slice: x: 4 (x_hi: 2, x_lo: 2; x = x_hi * 2 + x_lo), y: 4, z: 4, core: 2. Of those that a mesh axis runs over, the one named last changes fastest.
Arguments:
- tokens: bfloat16 [16384, 1024], P('dp'), may hold values from -6 to 6
- segment_ids: int32 [16384], P('dp'), may hold values from 0 to 7, as said below
- attn_gain: float32 [1024], replicated, may hold values from 0.25 to 1.75
- w_query: bfloat16 [1024, 1024], P(None, 'tensor'), may hold values from -0.1875 to 0.1875
- w_key: bfloat16 [1024, 512], P(None, 'tensor'), may hold values from -0.1875 to 0.1875
- w_value: bfloat16 [1024, 512], P(None, 'tensor'), may hold values from -0.1875 to 0.1875
- query_gain: float32 [64], replicated, may hold values from 0.25 to 1.75
- key_gain: float32 [64], replicated, may hold values from 0.25 to 1.75
- w_out: bfloat16 [1024, 1024], P('tensor'), may hold values from -1.5 to 1.5
- ffn_gain: float32 [1024], replicated, may hold values from 0.25 to 1.75
- w_gate: bfloat16 [1024, 4608], P(None, 'tensor'), may hold values from -0.1875 to 0.1875
- w_up: bfloat16 [1024, 4608], P(None, 'tensor'), may hold values from -0.1875 to 0.1875
- w_down: bfloat16 [4608, 1024], P('tensor'), may hold values from -0.1875 to 0.1875
- cotangent: bfloat16 [16384, 1024], P('dp'), may hold values from -6 to 6
Outputs:
- output: bfloat16 [16384, 1024], P('dp')
- input_grad: float32 [16384, 1024], P('dp')
- attn_gain_grad: float32 [1024], replicated
- w_query_grad: float32 [1024, 1024], P(None, 'tensor')
- w_key_grad: float32 [1024, 512], P(None, 'tensor')
- w_value_grad: float32 [1024, 512], P(None, 'tensor')
- query_gain_grad: float32 [64], replicated
- key_gain_grad: float32 [64], replicated
- w_out_grad: float32 [1024, 1024], P('tensor')
- ffn_gain_grad: float32 [1024], replicated
- w_gate_grad: float32 [1024, 4608], P(None, 'tensor')
- w_up_grad: float32 [1024, 4608], P(None, 'tensor')
- w_down_grad: float32 [4608, 1024], P('tensor')
Inputs may be any that keep to these rules, and one draw needn't show every extreme that they name: `segment_ids`: within each index of dp's 1024 tokens the ids start at 0 and never fall; a sequence is a run of equal ids and never crosses devices.
All inputs are finite; a program needn't handle non-finite values.
Results may differ from a plain program's by a relative error of at most 0.014.
The roundings to bfloat16 on the way count: a program that leaves them out, or rounds other values in their place, can miss the bound.
Values sent between devices are 32-bit elements; how exact they have to be, the bound alone decides.
No kernel may reach another device: no remote copies, remote signals or barrier semaphores. Data moves between devices by JAX's collectives and lax.ppermute only.
A program may use at most 128 MiB of HBM per device.

v0:
```python
import math
import jax
import jax.numpy as jnp
from jax import lax
from jax.sharding import PartitionSpec as P

EPS = 1e-05
THETA = 1000000.0


def outer(first_op, second_op):
    return lax.dot_general(
        first_op, second_op, (((0,), (0,)), ((), ())), preferred_element_type=jnp.float32
    )


def inner(first_op, second_op):
    return lax.dot_general(
        first_op, second_op, (((1,), (1,)), ((), ())), preferred_element_type=jnp.float32
    )


def rms_scale(values):
    return lax.rsqrt(jnp.mean(values * values, axis=-1, keepdims=True) + EPS)


def rms_back(upstream, values, inv_rms, gain_vec):
    normed = values * inv_rms
    weighted = upstream * gain_vec
    return inv_rms * (weighted - normed * jnp.mean(weighted * normed, axis=-1, keepdims=True))


def seq_layout(segment):
    length = segment.shape[0]
    ordinal = jnp.arange(length, dtype=jnp.int32)
    same_seq = segment[:, None] == segment[None, :]
    places = jnp.sum((same_seq & (ordinal[None, :] < ordinal[:, None])).astype(jnp.int32), axis=1)
    allowed = same_seq & (ordinal[None, :] <= ordinal[:, None])
    return (places, allowed)


def rope_tables(places, head_size):
    frequency = jnp.exp(
        jnp.arange(head_size // 2, dtype=jnp.float32) * (-2.0 * math.log(THETA) / head_size)
    )
    angles = places.astype(jnp.float32)[:, None] * frequency[None, :]
    angles = jnp.concatenate([angles, angles], axis=1)
    return (jnp.cos(angles), jnp.sin(angles))


def rotate(values, cosine, sine_table):
    half = values.shape[-1] // 2
    turned = jnp.concatenate([-values[..., half:], values[..., :half]], axis=-1)
    return values * cosine[:, None, :] + turned * sine_table[:, None, :]


def unrotate(incoming, cosine, sine_table):
    half = incoming.shape[-1] // 2
    scaled = incoming * sine_table[:, None, :]
    swapped = jnp.concatenate([scaled[..., half:], -scaled[..., :half]], axis=-1)
    return incoming * cosine[:, None, :] + swapped


def score_table(q_rot, k_rot, allowed, factor):
    raw = jnp.einsum("ikgd,jkd->kgij", q_rot, k_rot, preferred_element_type=jnp.float32) * factor
    return jnp.where(allowed[None, None], raw, -1e30)


def per_device(
    tokens,
    segment_ids,
    attn_gain,
    w_query,
    w_key,
    w_value,
    query_gain,
    key_gain,
    w_out,
    ffn_gain,
    w_gate,
    w_up,
    w_down,
    cotangent,
):
    length = tokens.shape[0]
    head_size = query_gain.shape[0]
    q_heads = w_query.shape[1] // head_size
    kv_heads = w_key.shape[1] // head_size
    groups = q_heads // kv_heads
    factor = 1.0 / math.sqrt(head_size)
    places, allowed = seq_layout(segment_ids)
    cosine, sine_table = rope_tables(places, head_size)
    tokens_wide = tokens.astype(jnp.float32)
    scale_one = rms_scale(tokens_wide)
    normed_one = (tokens_wide * scale_one * attn_gain).astype(jnp.bfloat16)
    q_raw = jnp.dot(normed_one, w_query, preferred_element_type=jnp.float32).reshape(
        length, q_heads, head_size
    )
    k_raw = jnp.dot(normed_one, w_key, preferred_element_type=jnp.float32).reshape(
        length, kv_heads, head_size
    )
    v_half = (
        jnp.dot(normed_one, w_value, preferred_element_type=jnp.float32)
        .astype(jnp.bfloat16)
        .reshape(length, kv_heads, head_size)
    )
    q_scale = rms_scale(q_raw)
    k_scale = rms_scale(k_raw)
    q_hat = q_raw * q_scale
    k_hat = k_raw * k_scale
    q_rot = (
        rotate(q_hat * query_gain, cosine, sine_table)
        .astype(jnp.bfloat16)
        .reshape(length, kv_heads, groups, head_size)
    )
    k_rot = rotate(k_hat * key_gain, cosine, sine_table).astype(jnp.bfloat16)
    scores = score_table(q_rot, k_rot, allowed, factor)
    row_peak = jnp.max(scores, axis=-1, keepdims=True)
    log_total = row_peak + jnp.log(jnp.sum(jnp.exp(scores - row_peak), axis=-1, keepdims=True))
    attn_probs = jnp.exp(scores - log_total).astype(jnp.bfloat16)
    attn_mixed = jnp.einsum(
        "kgij,jkd->ikgd", attn_probs, v_half, preferred_element_type=jnp.float32
    )
    attn_mixed = attn_mixed.reshape(length, q_heads * head_size).astype(jnp.bfloat16)
    attn_sum = lax.psum(jnp.dot(attn_mixed, w_out, preferred_element_type=jnp.float32), "tensor")
    residual = tokens_wide + attn_sum
    scale_two = rms_scale(residual)
    normed_two = (residual * scale_two * ffn_gain).astype(jnp.bfloat16)
    gate_proj = jnp.dot(normed_two, w_gate, preferred_element_type=jnp.float32)
    up_proj = jnp.dot(normed_two, w_up, preferred_element_type=jnp.float32)
    gate_sigmoid = jax.nn.sigmoid(gate_proj)
    hidden = (gate_proj * gate_sigmoid * up_proj).astype(jnp.bfloat16)
    mlp_sum = lax.psum(jnp.dot(hidden, w_down, preferred_element_type=jnp.float32), "tensor")
    output = (residual + mlp_sum).astype(jnp.bfloat16)
    down_grad = outer(hidden, cotangent)
    hidden_grad = inner(cotangent, w_down)
    gate_grad = (
        hidden_grad * up_proj * gate_sigmoid * (1.0 + gate_proj * (1.0 - gate_sigmoid))
    ).astype(jnp.bfloat16)
    up_grad = (hidden_grad * gate_proj * gate_sigmoid).astype(jnp.bfloat16)
    gate_w_grad = outer(normed_two, gate_grad)
    up_w_grad = outer(normed_two, up_grad)
    normed_two_grad = lax.psum(inner(gate_grad, w_gate) + inner(up_grad, w_up), "tensor")
    ffn_grad = jnp.sum(normed_two_grad * residual * scale_two, axis=0)
    residual_grad = cotangent.astype(jnp.float32) + rms_back(
        normed_two_grad, residual, scale_two, ffn_gain
    )
    residual_half = residual_grad.astype(jnp.bfloat16)
    out_w_grad = outer(attn_mixed, residual_half)
    mixed_grad = (
        inner(residual_half, w_out)
        .astype(jnp.bfloat16)
        .reshape(length, kv_heads, groups, head_size)
    )
    attn_full = jnp.exp(score_table(q_rot, k_rot, allowed, factor) - log_total)
    probs_half = attn_full.astype(jnp.bfloat16)
    value_grad = jnp.einsum(
        "kgij,ikgd->jkd", probs_half, mixed_grad, preferred_element_type=jnp.float32
    ).astype(jnp.bfloat16)
    prob_grad = jnp.einsum("ikgd,jkd->kgij", mixed_grad, v_half, preferred_element_type=jnp.float32)
    row_delta = jnp.sum(attn_full * prob_grad, axis=-1, keepdims=True)
    score_grad = (attn_full * (prob_grad - row_delta) * factor).astype(jnp.bfloat16)
    q_rot_grad = jnp.einsum(
        "kgij,jkd->ikgd", score_grad, k_rot, preferred_element_type=jnp.float32
    ).reshape(length, q_heads, head_size)
    k_rot_grad = jnp.einsum("kgij,ikgd->jkd", score_grad, q_rot, preferred_element_type=jnp.float32)
    q_norm_grad = unrotate(q_rot_grad, cosine, sine_table)
    k_norm_grad = unrotate(k_rot_grad, cosine, sine_table)
    qgain_grad = jnp.sum(q_norm_grad * q_hat, axis=(0, 1))
    kgain_grad = jnp.sum(k_norm_grad * k_hat, axis=(0, 1))
    qgain_grad, kgain_grad = lax.psum((qgain_grad, kgain_grad), ("dp", "tensor"))
    q_grad = (
        rms_back(q_norm_grad, q_raw, q_scale, query_gain)
        .astype(jnp.bfloat16)
        .reshape(length, q_heads * head_size)
    )
    k_grad = (
        rms_back(k_norm_grad, k_raw, k_scale, key_gain)
        .astype(jnp.bfloat16)
        .reshape(length, kv_heads * head_size)
    )
    v_grad = value_grad.reshape(length, kv_heads * head_size)
    query_w_grad = outer(normed_one, q_grad)
    key_w_grad = outer(normed_one, k_grad)
    value_w_grad = outer(normed_one, v_grad)
    normed_one_grad = lax.psum(
        inner(q_grad, w_query) + inner(k_grad, w_key) + inner(v_grad, w_value), "tensor"
    )
    attn_grad = jnp.sum(normed_one_grad * tokens_wide * scale_one, axis=0)
    input_grad = residual_grad + rms_back(normed_one_grad, tokens_wide, scale_one, attn_gain)
    (
        attn_grad,
        query_w_grad,
        key_w_grad,
        value_w_grad,
        out_w_grad,
        ffn_grad,
        gate_w_grad,
        up_w_grad,
        down_grad,
    ) = lax.psum(
        (
            attn_grad,
            query_w_grad,
            key_w_grad,
            value_w_grad,
            out_w_grad,
            ffn_grad,
            gate_w_grad,
            up_w_grad,
            down_grad,
        ),
        "dp",
    )
    return (
        output,
        input_grad,
        attn_grad,
        query_w_grad,
        key_w_grad,
        value_w_grad,
        qgain_grad,
        kgain_grad,
        out_w_grad,
        ffn_grad,
        gate_w_grad,
        up_w_grad,
        down_grad,
    )


def solution(mesh):
    return jax.shard_map(
        per_device,
        mesh=mesh,
        in_specs=(
            P("dp", None),
            P("dp"),
            P(),
            P(None, "tensor"),
            P(None, "tensor"),
            P(None, "tensor"),
            P(),
            P(),
            P("tensor", None),
            P(),
            P(None, "tensor"),
            P(None, "tensor"),
            P("tensor", None),
            P("dp", None),
        ),
        out_specs=(
            P("dp", None),
            P("dp", None),
            P(),
            P(None, "tensor"),
            P(None, "tensor"),
            P(None, "tensor"),
            P(),
            P(),
            P("tensor", None),
            P(),
            P(None, "tensor"),
            P(None, "tensor"),
            P("tensor", None),
        ),
        check_vma=False,
    )
```

profile of v0, /device:TPU:0, one launch (start us, length us, event | category | flops | bytes accessed | tf_op | source)
XLA Modules:
  0.0 972.6 jit_solution(14116732110158789731)
XLA Ops:
  9.1 2.3 compare_and_fusion.1
  11.4 2.1 fusion.15
  23.2 1.9 fusion.33
  29.8 2.0 exponential_reduce_fusion
  33.1 2.4 convolution_convert_fusion.1
  36.2 2.7 fusion.55
  39.6 186.9 %all-reduce.9.cloned.1.call-done = f32[1024,1024]{1,0:T(8,128)} async-done(((f32[1024,1024]{1,0:T(8,128)}), f32[1024,1024]{1,0:T(8,128)}) %all-reduce.9.cloned.1.call-update) | async-done | bytes 4194320 | tf_op jit(solution)/shard_map/psum | solution.py:125
  226.4 3.5 multiply_reduce_fusion.2
  235.8 3.4 multiply_convert_fusion.1
  241.0 3.9 convolution_add_fusion
  245.2 5.1 fusion.58
  250.3 178.7 %all-reduce.11.cloned.1.call-done = f32[1024,1024]{1,0:T(8,128)} async-done(((f32[1024,1024]{1,0:T(8,128)}), f32[1024,1024]{1,0:T(8,128)}) %all-reduce.11.cloned.1.call-update) | async-done | bytes 4194320 | tf_op jit(solution)/shard_map/psum | solution.py:143
  429.0 5.4 multiply_reduce_fusion
  434.4 3.7 multiply_add_fusion
  438.1 1.9 copy-done.5
  441.3 3.0 fusion
  444.3 2.5 fusion.20
  446.8 3.1 fusion.18
  451.3 2.0 fusion.40
  457.1 2.7 add_add_fusion
  459.9 4.9 fusion.66
  464.8 2.8 fusion.67
  467.6 2.8 fusion.63
  476.3 328.4 %all-reduce = (f32[64]{0:T(128)}, f32[64]{0:T(128)}) all-reduce(f32[64]{0:T(128)S(1)} %copy-done.63, f32[64]{0:T(128)S(1)} %get-tuple-element.19), channel_id=1, replica_groups=mesh['dp'=16,'tensor'=8] {'dp','tensor'}, use_global_device_ids=true, to_apply=%region_22.23 | all-reduce | flops 128 | bytes 1024 | tf_op jit(solution)/shard_map/psum | solution.py:171
  804.7 3.6 fusion.17
  808.3 31.5 %all-reduce.1 = (f32[1024]{0:T(1024)}, f32[1024]{0:T(1024)}) all-reduce(f32[1024]{0:T(1024)S(1)} %get-tuple-element.15, f32[1024]{0:T(1024)S(1)} %copy-done.57), channel_id=1, replica_groups=mesh['dp'=16,'tensor'=8] {'dp'}, use_global_device_ids=true, to_apply=%region_17.18 | all-reduce | flops 2048 | bytes 16384 | tf_op jit(solution)/shard_map/psum | solution.py:201
  839.8 5.9 add_convert_fusion
  846.8 2.7 fusion.13
  849.4 102.6 %all-reduce.13.cloned.1.call-done = (f32[1024,128]{1,0:T(8,128)}, f32[1024,64]{0,1:T(8,128)}, f32[1024,64]{0,1:T(8,128)}, f32[128,1024]{1,0:T(8,128)}, f32[1024,...) async-done(((f32[1024,128]{1,0:T(8,128)}, f32[1024,64]{0,1:T(8,128)}, f32[1024,64]{0,1:T(8,128)}, f32[128,1024]{1,0:T(8,128)}, f32[1024,576]{0,1:T(8,128)}, ...) | async-done | bytes 8650768 | tf_op jit(solution)/shard_map/psum | solution.py:201
  952.1 2.0 copy.46
  957.4 1.9 copy.49
  959.3 3.5 copy.50
  (195 shorter events, 45.8 us)
Async XLA Ops:
  7.2 228.4 %copy-start = (bf16[576,1024]{1,0:T(8,128)(2,1)S(1)}, bf16[576,1024]{1,0:T(8,128)(2,1)}, u32[]{:S(2)}) copy-start(bf16[576,1024]{1,0:T(8,128)(2,1)} %param.26) | copy-start | bytes 3538948
  7.2 219.2 %all-reduce.9.cloned.1.call-start = ((), (), s32[]{:S(2)}) async-start(), calls=%async_computation | async-start | bytes 8388608 | tf_op jit(solution)/shard_map/psum | solution.py:125
  7.2 6.3 copy-start.8
  7.3 7.6 copy-start.47
  11.4 4.2 copy-start.58
  13.6 3.8 copy-start.53
  14.9 3.3 copy-start.61
  21.7 6.2 copy-start.10
  25.1 4.6 copy-start.49
  31.8 3.7 copy-start.51
  39.0 390.0 %all-reduce.11.cloned.1.call-start = ((), (), s32[]{:S(2)}) async-start(), calls=%async_computation.1 | async-start | bytes 8388608 | tf_op jit(solution)/shard_map/psum | solution.py:143
  229.9 3.7 copy-start.2
  244.9 559.7 %all-reduce.15.cloned.1.call-start = ((), (), s32[]{:S(2)}) async-start(), calls=%async_computation.3 | async-start | bytes 16777216 | tf_op jit(solution)/shard_map/psum | solution.py:133
  250.3 184.1 %copy-start.55 = (f32[1024]{0:T(1024)S(1)}, f32[1024]{0:T(1024)}, u32[]{:S(2)}) copy-start(f32[1024]{0:T(1024)} %param.23) | copy-start | bytes 12292
  429.0 5.4 copy-start.3
  429.0 11.9 %slice-start = ((s8[8388608]{0:T(1024)(128)(4,1)}), s8[4194304]{0:T(1024)(128)(4,1)S(1)}, s32[]{:S(2)}) async-start(s8[8388608]{0:T(1024)(128)(4,1)} %bitcast.195), calls=%async_computation.4 | async-start | bytes 8388608
  434.4 5.7 copy-start.36
  434.4 6.5 slice-start.1
  446.8 10.3 %copy-start.43 = (bf16[1024,64]{0,1:T(8,128)(2,1)}, bf16[1024,64]{0,1:T(8,128)(2,1)S(1)}, u32[]{:S(2)}) copy-start(bf16[1024,64]{0,1:T(8,128)(2,1)S(1)} %fusion.20) | copy-start | bytes 393220
  459.8 5.0 copy-start.24
  459.8 492.2 %all-reduce.13.cloned.1.call-start = ((), (), s32[]{:S(2)}) async-start(), calls=%async_computation.2 | async-start | bytes 17301504 | tf_op jit(solution)/shard_map/psum | solution.py:201
  459.9 4.9 copy-start.28
  467.6 4.0 copy-start.33
  475.6 329.0 %copy-start.9 = (bf16[1024,1024]{1,0:T(8,128)(2,1)S(1)}, bf16[1024,1024]{1,0:T(8,128)(2,1)}, u32[]{:S(2)}) copy-start(bf16[1024,1024]{1,0:T(8,128)(2,1)} %param.14) | copy-start | bytes 6291460
  475.6 329.0 %copy-start.54 = (f32[1024]{0:T(1024)S(1)}, f32[1024]{0:T(1024)}, u32[]{:S(2)}) copy-start(f32[1024]{0:T(1024)} %copy-done.53) | copy-start | bytes 12292
  475.6 329.0 %copy-start.56 = (f32[1024]{0:T(1024)S(1)}, f32[1024]{0:T(1024)}, u32[]{:S(2)}) copy-start(f32[1024]{0:T(1024)} %param.16) | copy-start | bytes 12292
  475.7 332.6 %copy-start.57 = (f32[1024]{0:T(1024)S(1)}, f32[1024]{0:T(1024)}, u32[]{:S(2)}) copy-start(f32[1024]{0:T(1024)} %get-tuple-element.13) | copy-start | bytes 12292
  839.8 5.9 copy-start.7
  839.8 7.0 copy-start.14
  952.1 10.8 %copy-start.26 = (f32[1024,576]{0,1:T(8,128)S(1)}, f32[1024,576]{0,1:T(8,128)}, u32[]{:S(2)}) copy-start(f32[1024,576]{0,1:T(8,128)} %get-tuple-element.77) | copy-start | bytes 7077892
  959.3 4.9 copy-start.25
  959.3 6.3 copy-start.1
  (41 other events, 81.6 us)
Sparse Core Ops, SparseCore 0:
  39.1 187.2 all-reduce.8
  245.1 183.8 all-reduce.10
  459.9 343.1 all-reduce.14
  807.3 144.7 all-reduce.12
where the time goes:
time: 981 us; the launch traced here: 973 us
  waiting for transfers between devices  468 us (48%)
  blocking collectives  360 us (37%)
  matrix products  55.6 us (6%)
  other arithmetic  48.5 us (5%)
  local copies, waits for them, and re-layouts  24.5 us (2%)
  between operations  15 us (2%)
    psum x1, blocking collectives, per_device(): lax.psum((qgain_grad, kgain_grad), ('dp', 'tensor'))  328 us
    psum x1, waiting for transfers between devices, per_device(): lax.psum(jnp.dot(attn_mixed, w_out, preferred_element_type=jnp.float32),...  187 us
    psum x1, waiting for transfers between devices, per_device(): lax.psum(inner(gate_grad, w_gate) + inner(up_grad, w_up), 'tensor')  179 us
    psum x1, waiting for transfers between devices, per_device(): lax.psum((attn_grad, query_w_grad, key_w_grad, value_w_grad, out_w_grad,...  103 us
    psum x1, blocking collectives, per_device(): lax.psum((attn_grad, query_w_grad, key_w_grad, value_w_grad, out_w_grad,...  31.5 us
    unnamed x145, local copies, waits for them, and re-layouts  22.7 us
  transfers between devices with their start and end apart: 4, of which 3 were waited for; matrix products, arithmetic and copies ran while one was open for 3% of the time, Pallas kernels for 0%

commit v1 on v0

--- a/solution.py
+++ b/solution.py
@@ -122,7 +122,9 @@
         "kgij,jkd->ikgd", attn_probs, v_half, preferred_element_type=jnp.float32
     )
     attn_mixed = attn_mixed.reshape(length, q_heads * head_size).astype(jnp.bfloat16)
-    attn_sum = lax.psum(jnp.dot(attn_mixed, w_out, preferred_element_type=jnp.float32), "tensor")
+    xs = jnp.dot(attn_mixed, w_out, preferred_element_type=jnp.float32)
+    all_values = jax.lax.all_gather(xs, "tensor")
+    attn_sum = jnp.sum(all_values, 0)
     residual = tokens_wide + attn_sum
     scale_two = rms_scale(residual)
     normed_two = (residual * scale_two * ffn_gain).astype(jnp.bfloat16)

time: 981 us -> 1140 us (1.16)
  waiting for transfers between devices: 468 us -> 617 us
    all_gather x0 -> x1, waiting for transfers between devices: none -> 336 us  [per_device(): all_values = jax.lax.all_gather(xs, 'tensor')]
    psum x1 -> x0, waiting for transfers between devices: 187 us -> none  [per_device(): lax.psum(jnp.dot(attn_mixed, w_out, preferred_element_type=jnp.float32),...]
    reduce_sum x0 -> x1, other arithmetic: none -> 14.7 us  [per_device(): attn_sum = jnp.sum(all_values, 0)]
    unnamed x145 -> x155, local copies, waits for them, and re-layouts: 22.7 us -> 24.7 us
where the time goes in v1:
time: 1140 us; the launch traced here: 1130 us
  waiting for transfers between devices  617 us (54%)
  blocking collectives  358 us (31%)
  other arithmetic  57.6 us (5%)
  matrix products  55.3 us (5%)
  local copies, waits for them, and re-layouts  25.4 us (2%)
  between operations  15.1 us (1%)
    all_gather x1, waiting for transfers between devices, per_device(): all_values = jax.lax.all_gather(xs, 'tensor')  336 us
    psum x1, blocking collectives, per_device(): lax.psum((qgain_grad, kgain_grad), ('dp', 'tensor'))  329 us
    psum x1, waiting for transfers between devices, per_device(): lax.psum(inner(gate_grad, w_gate) + inner(up_grad, w_up), 'tensor')  178 us
    psum x1, waiting for transfers between devices, per_device(): lax.psum((attn_grad, query_w_grad, key_w_grad, value_w_grad, out_w_grad,...  104 us
    psum x1, blocking collectives, per_device(): lax.psum((attn_grad, query_w_grad, key_w_grad, value_w_grad, out_w_grad,...  29.3 us
    unnamed x155, local copies, waits for them, and re-layouts  24.7 us
  transfers between devices with their start and end apart: 4, of which 3 were waited for; matrix products, arithmetic and copies ran while one was open for 3% of the time, Pallas kernels for 0%

profile of v1, /device:TPU:0, one launch (start us, length us, event | category | flops | bytes accessed | tf_op | source)
XLA Modules:
  0.0 1129.6 jit_solution(1236147289378812340)
XLA Ops:
  9.0 2.4 compare_and_fusion.1
  12.1 2.1 fusion.15
  14.2 2.2 fusion.9
  24.0 2.0 exponential_reduce_fusion
  27.2 2.4 convolution_convert_fusion.1
  30.4 2.7 fusion.55
  33.7 336.0 %all-gather.3.cloned.1.call-done = f32[8192,1024]{1,0:T(8,128)} async-done(((f32[1024,1024]{1,0:T(8,128)}), f32[8192,1024]{1,0:T(8,128)}) %all-gather.3.cloned.1.call-update) | async-done | bytes 33554448 | tf_op jit(solution)/shard_map/all_gather | solution.py:126
  369.8 14.7 %reduce_sum.149 = f32[1024,1024]{1,0:T(8,128)} reduce(f32[8,1024,1024]{2,1,0:T(8,128)} %bitcast.198, f32[]{:T(128)} %constant.10.clone.1), dimensions={0}, to_apply=%region_6.7 | reduce | flops 7340032 | bytes 37748740 | tf_op jit(solution)/shard_map/reduce_sum | solution.py:127
  384.4 3.5 multiply_reduce_fusion.2
  393.7 3.3 multiply_convert_fusion.1
  398.9 4.0 convolution_add_fusion
  403.2 5.1 fusion.58
  408.3 177.6 %all-reduce.8.cloned.1.call-done = f32[1024,1024]{1,0:T(8,128)} async-done(((f32[1024,1024]{1,0:T(8,128)}), f32[1024,1024]{1,0:T(8,128)}) %all-reduce.8.cloned.1.call-update) | async-done | bytes 4194320 | tf_op jit(solution)/shard_map/psum | solution.py:145
  585.9 5.4 multiply_reduce_fusion
  591.3 3.7 multiply_add_fusion
  595.0 2.0 copy-done.5
  598.2 2.5 fusion.20
  600.8 3.0 fusion
  603.8 3.1 fusion.18
  608.2 2.0 fusion.40
  614.1 2.7 add_add_fusion
  618.0 4.5 fusion.67
  622.6 2.8 fusion.66
  625.4 2.8 fusion.63
  634.1 328.8 %all-reduce = (f32[64]{0:T(128)}, f32[64]{0:T(128)}) all-reduce(f32[64]{0:T(128)S(1)} %copy-done.67, f32[64]{0:T(128)S(1)} %get-tuple-element.19), channel_id=1, replica_groups=mesh['dp'=16,'tensor'=8] {'dp','tensor'}, use_global_device_ids=true, to_apply=%region_22.23 | all-reduce | flops 128 | bytes 1024 | tf_op jit(solution)/shard_map/psum | solution.py:173
  962.9 3.6 fusion.17
  966.5 29.3 %all-reduce.1 = (f32[1024]{0:T(1024)}, f32[1024]{0:T(1024)}) all-reduce(f32[1024]{0:T(1024)S(1)} %get-tuple-element.15, f32[1024]{0:T(1024)S(1)} %copy-done.59), channel_id=1, replica_groups=mesh['dp'=16,'tensor'=8] {'dp'}, use_global_device_ids=true, to_apply=%region_17.18 | all-reduce | flops 2048 | bytes 16384 | tf_op jit(solution)/shard_map/psum | solution.py:203
  995.8 5.8 add_convert_fusion
  1002.8 2.7 fusion.13
  1005.5 103.6 %all-reduce.10.cloned.1.call-done = (f32[1024,128]{1,0:T(8,128)}, f32[1024,64]{0,1:T(8,128)}, f32[1024,64]{0,1:T(8,128)}, f32[128,1024]{1,0:T(8,128)}, f32[1024,...) async-done(((f32[1024,128]{1,0:T(8,128)}, f32[1024,64]{0,1:T(8,128)}, f32[1024,64]{0,1:T(8,128)}, f32[128,1024]{1,0:T(8,128)}, f32[1024,576]{0,1:T(8,128)}, ...) | async-done | bytes 8650768 | tf_op jit(solution)/shard_map/psum | solution.py:203
  1109.1 2.0 copy.45
  1116.3 3.5 copy.49
  (206 shorter events, 42.7 us)
Async XLA Ops:
  7.2 386.4 %copy-start = (bf16[576,1024]{1,0:T(8,128)(2,1)S(1)}, bf16[576,1024]{1,0:T(8,128)(2,1)}, u32[]{:S(2)}) copy-start(bf16[576,1024]{1,0:T(8,128)(2,1)} %param.26) | copy-start | bytes 3538948
  7.2 9.2 copy-start.42
  7.2 362.6 %all-gather.3.cloned.1.call-start = ((), (), s32[]{:S(2)}) async-start(), calls=%async_computation.1 | async-start | bytes 37748736 | tf_op jit(solution)/shard_map/all_gather | solution.py:126
  12.1 9.2 copy-start.62
  12.1 5.1 copy-start.48
  14.2 3.8 copy-start.54
  14.2 3.8 copy-start.60
  14.2 3.9 copy-start.40
  17.2 8.8 copy-start.44
  18.2 4.0 copy-start.9
  33.1 552.7 %all-reduce.8.cloned.1.call-start = ((), (), s32[]{:S(2)}) async-start(), calls=%async_computation | async-start | bytes 8388608 | tf_op jit(solution)/shard_map/psum | solution.py:145
  387.9 3.6 copy-start.2
  403.0 559.9 %all-reduce.12.cloned.1.call-start = ((), (), s32[]{:S(2)}) async-start(), calls=%async_computation.3 | async-start | bytes 16777216 | tf_op jit(solution)/shard_map/psum | solution.py:135
  408.3 183.0 %copy-start.57 = (f32[1024]{0:T(1024)S(1)}, f32[1024]{0:T(1024)}, u32[]{:S(2)}) copy-start(f32[1024]{0:T(1024)} %param.23) | copy-start | bytes 12292
  585.9 5.4 copy-start.3
  585.9 12.0 %slice-start = ((s8[8388608]{0:T(1024)(128)(4,1)}), s8[4194304]{0:T(1024)(128)(4,1)S(1)}, s32[]{:S(2)}) async-start(s8[8388608]{0:T(1024)(128)(4,1)} %bitcast.196), calls=%async_computation.4 | async-start | bytes 8388608
  591.2 5.7 copy-start.37
  591.3 6.6 slice-start.1
  600.8 13.3 %copy-start.46 = (bf16[1024,64]{0,1:T(8,128)(2,1)}, bf16[1024,64]{0,1:T(8,128)(2,1)S(1)}, u32[]{:S(2)}) copy-start(bf16[1024,64]{0,1:T(8,128)(2,1)S(1)} %fusion.20) | copy-start | bytes 393220
  616.8 492.3 %all-reduce.10.cloned.1.call-start = ((), (), s32[]{:S(2)}) async-start(), calls=%async_computation.2 | async-start | bytes 17301504 | tf_op jit(solution)/shard_map/psum | solution.py:203
  618.0 4.5 copy-start.29
  618.0 4.5 copy-start.71
  625.4 4.0 copy-start.34
  633.5 329.5 %copy-start.8 = (bf16[1024,1024]{1,0:T(8,128)(2,1)S(1)}, bf16[1024,1024]{1,0:T(8,128)(2,1)}, u32[]{:S(2)}) copy-start(bf16[1024,1024]{1,0:T(8,128)(2,1)} %param.14) | copy-start | bytes 6291460
  633.5 329.5 %copy-start.55 = (f32[1024]{0:T(1024)S(1)}, f32[1024]{0:T(1024)}, u32[]{:S(2)}) copy-start(f32[1024]{0:T(1024)} %copy-done.54) | copy-start | bytes 12292
  633.5 329.5 %copy-start.58 = (f32[1024]{0:T(1024)S(1)}, f32[1024]{0:T(1024)}, u32[]{:S(2)}) copy-start(f32[1024]{0:T(1024)} %param.16) | copy-start | bytes 12292
  633.5 333.0 %copy-start.59 = (f32[1024]{0:T(1024)S(1)}, f32[1024]{0:T(1024)}, u32[]{:S(2)}) copy-start(f32[1024]{0:T(1024)} %get-tuple-element.13) | copy-start | bytes 12292
  995.8 5.9 copy-start.7
  995.8 7.0 copy-start.13
  1109.0 10.8 copy-start.27
  1116.3 4.9 copy-start.26
  1116.3 6.3 copy-start.1
  (46 other events, 94.3 us)
Sparse Core Ops, SparseCore 0:
  33.3 336.4 all-gather.2
  403.1 182.7 all-reduce.7
  616.9 343.2 all-reduce.11
  964.3 144.7 all-reduce.9
